TPU v7x, 32 devices: a whole 2x2x4 slice. The times are simulated.
32 devices in a mesh: harm: 4 (over y, x), slab: 8 (over z, core).
Axes of the slice: x: 2, y: 2, z: 4, core: 2. Of those that a mesh axis runs over, the one named last changes fastest.
Arguments:
- krylov_basis: float32 [3, 4, 4, 16, 32, 128], P(None, 'harm', None, 'slab'), may hold values from -16 to 16
- weights: float32 [3], replicated, may hold values from -3 to 3
- base_flow: bfloat16 [4, 3, 16, 32, 128], P('harm', None, 'slab'), may hold values from -4 to 4
- shifts: float32 [4], P('harm'), may hold values from 0.25 to 2
Outputs:
- next_vector: float32 [4, 4, 16, 32, 128], P('harm', None, 'slab')
- arnoldi_column: float32 [4], replicated
All inputs are finite; a program needn't handle non-finite values.
Results may differ from a plain program's by a relative error of at most 0.009.
Values may be sent and summed in bfloat16 or wider, within the bound.
No kernel may reach another device: no remote copies, remote signals or barrier semaphores. Data moves between devices by JAX's collectives and lax.ppermute only.
A program may use at most 64 MiB of HBM per device.

v0:
```python
import jax
import jax.numpy as jnp
from jax import lax
from jax.sharding import PartitionSpec as P

SWEEPS = 4
viscosity = 1.0
epsilon = 1e-06


def padded_2(cells, sides, width):
    for axis, dim in sides:
        count = lax.axis_size(axis)
        ends = count - 1
        head = lax.slice_in_dim(cells, 0, width, axis=dim)
        tail = lax.slice_in_dim(cells, cells.shape[dim] - width, cells.shape[dim], axis=dim)
        cells = jnp.concatenate(
            [
                lax.ppermute(tail, axis, [(i, (i + 1) % count) for i in range(ends)]),
                cells,
                lax.ppermute(head, axis, [((i + 1) % count, i) for i in range(ends)]),
            ],
            axis=dim,
        )
    return cells


def broadcast(x, axis, root):
    mine = lax.axis_index(axis) == root
    return lax.psum(jnp.where(mine, x, jnp.zeros_like(x)), axis)


def shifted(value, axis, steps):
    count = lax.axis_size(axis)
    pairs = [(source, (source + steps) % count) for source in range(count)]
    return lax.ppermute(value, axis, pairs)


def neighbours_y(values):
    padded = jnp.pad(values, ((0, 0), (0, 0), (1, 1), (0, 0)))
    return (padded[:, :, 2:], padded[:, :, :-2])


def laplace_ext(extended):
    center = extended[:, 1:-1]
    upper_y, lower_y = neighbours_y(center)
    result = extended[:, 2:] + extended[:, :-2] + upper_y + lower_y
    result = result + jnp.roll(center, -1, axis=3) + jnp.roll(center, 1, axis=3)
    return result - 6.0 * center


def divergence_split(flux_x, flux_y, flux_z):
    upper_y, lower_y = neighbours_y(flux_y)
    result = 0.5 * (flux_x[:, 2:] - flux_x[:, :-2])
    result = result + 0.5 * (upper_y - lower_y)
    return result + 0.5 * (jnp.roll(flux_z, -1, axis=3) - jnp.roll(flux_z, 1, axis=3))


def sweep_extend(values):
    return padded_2(values, (("slab", 1),), 1)


def chebyshev(applied, shift_value):
    middle = shift_value + 6.0 * viscosity
    half_span = 6.0 * viscosity
    span_ratio = middle / half_span
    solution = jnp.zeros_like(applied)
    remainder = applied
    direction = applied / middle
    ratio_prev = 1.0 / span_ratio
    for sweep_index in range(SWEEPS):
        solution = solution + direction
        remainder = remainder - (
            shift_value * direction - viscosity * laplace_ext(sweep_extend(direction))
        )
        ratio_next = 1.0 / (2.0 * span_ratio - ratio_prev)
        direction = ratio_next * ratio_prev * direction + 2.0 * ratio_next / half_span * remainder
        ratio_prev = ratio_next
    return solution + direction


def shards(krylov_basis, weights, base_flow, shifts):
    vectors = krylov_basis[:, 0]
    start_vec = jnp.sum(weights[:, None, None, None, None] * vectors, axis=0)
    harm_count = lax.axis_size("harm") * base_flow.shape[0]
    local_flow = base_flow[0]
    cell_shape = start_vec.shape
    empty = jnp.zeros((3,) + cell_shape, jnp.float32)

    def add_term(fluxes, current, cycle_step):
        shared = broadcast(local_flow, "harm", cycle_step).astype(jnp.float32)
        return fluxes + shared[:, None] * current[None]

    def advance(cycle_step, carried):
        fluxes, current = carried
        fluxes = add_term(fluxes, current, cycle_step)
        return (fluxes, shifted(current, "harm", 1))

    fluxes, current = lax.fori_loop(0, harm_count - 1, advance, (empty, start_vec))
    fluxes = add_term(fluxes, current, harm_count - 1)
    fluxes = fluxes.reshape((12,) + cell_shape[1:])
    stacked = jnp.concatenate([fluxes, start_vec], axis=0)
    extended = padded_2(stacked, (("slab", 1),), 1)
    moved = divergence_split(extended[0:4], extended[4:8, 1:-1], extended[8:12, 1:-1])
    field_ext = extended[12:]
    own_shift = shifts[0]
    applied = own_shift * start_vec - viscosity * laplace_ext(field_ext) + moved
    solution = chebyshev(applied, own_shift)
    entries = float(
        harm_count
        * cell_shape[0]
        * cell_shape[1]
        * lax.axis_size("slab")
        * cell_shape[2]
        * cell_shape[3]
    )
    local_proj = jnp.sum(vectors * solution[None], axis=(1, 2, 3, 4))
    projection = lax.psum(local_proj, ("harm", "slab")) / entries
    residue = solution - jnp.sum(projection[:, None, None, None, None] * vectors, axis=0)
    square = lax.psum(jnp.sum(residue * residue), ("harm", "slab")) / entries
    norm_value = jnp.sqrt(square + epsilon)
    next_vector = (residue / norm_value)[None]
    arnoldi_column = jnp.concatenate([projection, norm_value[None]])
    return (next_vector, arnoldi_column)


def solution(mesh):
    in_specs = (
        P(None, "harm", None, "slab", None, None),
        P(),
        P("harm", None, "slab", None, None),
        P("harm"),
    )
    out_specs = (P("harm", None, "slab", None, None), P())
    return jax.shard_map(shards, mesh=mesh, in_specs=in_specs, out_specs=out_specs, check_vma=False)
```

profile of v0, /device:TPU:0, one launch (start us, length us, event | category | flops | bytes accessed | tf_op | source)
XLA Modules:
  0.0 199.5 jit_solution(12436300417976476142)
XLA Ops:
  0.7 0.6 copy-done.5
  1.3 1.1 fusion
  2.4 0.6 copy-done
  3.1 0.2 copy-done.4
  3.3 18.4 %psum.32 = bf16[3,2,32,128]{3,2,1,0:T(8,128)(2,1)S(1)} all-reduce(bf16[3,2,32,128]{3,2,1,0:T(8,128)(2,1)S(1)} %broadcast_select_fusion.1), channel_id=1, replica_groups=mesh['harm'=4,'slab'=8] {'harm'}, use_global_device_ids=true, to_apply=%region_4.5 | all-reduce | flops 24576 | bytes 98304 | tf_op jit(solution)/shard_map/psum | solution.py:30
  21.7 52.6 %while.16 = (s32[]{:T(128)}, f32[3,4,2,32,128]{4,3,2,1,0:T(8,128)S(1)}, f32[4,2,32,128]{3,2,1,0:T(8,128)S(1)}, bf16[3,2,32,128]{3,2,1,0:T(8,128)(2,1)S(1)}, s32[]{:T(128)}, /*index=5*/u32[]{:T(128)}, s32[]{:T(128)}) while((s32[]{:T(128)}, f32[3,4,2,32,128]{4,3,2,1,0:T(8,128)S(1)}, f32[4,2,32,128]{3,2,1,0:T(8,128)S(1)}, ...), condition=%wide.region_3.4_spmd.clone, body=%wide.region_1.3_spmd.clone.sunk | while | flops 368647 | bytes 2146473 | solution.py:99
  21.8 17.2 %psum.37 = bf16[3,2,32,128]{3,2,1,0:T(8,128)(2,1)S(1)} all-reduce(bf16[3,2,32,128]{3,2,1,0:T(8,128)(2,1)S(1)} %broadcast_select_fusion.3), channel_id=1, replica_groups=mesh['harm'=4,'slab'=8] {'harm'}, use_global_device_ids=true, to_apply=%region_2.2 | all-reduce | flops 24576 | bytes 98304 | tf_op jit(solution)/shard_map/while/body/eval_jaxpr/psum | solution.py:30
  39.4 17.3 %psum.37 = bf16[3,2,32,128]{3,2,1,0:T(8,128)(2,1)S(1)} all-reduce(bf16[3,2,32,128]{3,2,1,0:T(8,128)(2,1)S(1)} %broadcast_select_fusion.3), channel_id=1, replica_groups=mesh['harm'=4,'slab'=8] {'harm'}, use_global_device_ids=true, to_apply=%region_2.2 | all-reduce | flops 24576 | bytes 98304 | tf_op jit(solution)/shard_map/while/body/eval_jaxpr/psum | solution.py:30
  56.9 17.1 %psum.37 = bf16[3,2,32,128]{3,2,1,0:T(8,128)(2,1)S(1)} all-reduce(bf16[3,2,32,128]{3,2,1,0:T(8,128)(2,1)S(1)} %broadcast_select_fusion.3), channel_id=1, replica_groups=mesh['harm'=4,'slab'=8] {'harm'}, use_global_device_ids=true, to_apply=%region_2.2 | all-reduce | flops 24576 | bytes 98304 | tf_op jit(solution)/shard_map/while/body/eval_jaxpr/psum | solution.py:30
  74.3 0.8 copy-done.1
  75.2 1.3 collective-permute-start.1
  76.5 3.0 %collective-permute-start.2 = (f32[16,1,32,128]{3,2,1,0:T(8,128)S(1)}, f32[16,1,32,128]{3,2,1,0:T(8,128)S(1)}, u32[]{:S(2)}, u32[]{:S(2)}) collective-permute-start(f32[16,1,32,128]{3,2,1,0:T(8,128)S(1)} %get-tuple-element.118), channel_id=1, source_target_pairs={{0,1},{1,2},{2,3},{3,4},{4,5},{5,6},{6,7},{8,9},{9,10},{10,11},{11... | collective-permute-start | bytes 786440 | tf_op jit(solution)/shard_map/ppermute | solution.py:19
  80.9 0.2 broadcast_divide_fusion
  81.2 1.3 collective-permute-start.3
  82.5 5.7 %collective-permute-start.4 = (f32[4,1,32,128]{3,2,1,0:T(8,128)S(1)}, f32[4,1,32,128]{3,2,1,0:T(8,128)S(1)}, u32[]{:S(2)}, u32[]{:S(2)}) collective-permute-start(f32[4,1,32,128]{3,2,1,0:T(8,128)S(1)} %get-tuple-element.140), channel_id=1, source_target_pairs={{0,1},{1,2},{2,3},{3,4},{4,5},{5,6},{6,7},{8,9},{9,10},{10,11},{11... | collective-permute-start | bytes 196616 | tf_op jit(solution)/shard_map/ppermute | solution.py:19
  88.3 0.8 collective-permute-done.4
  89.4 1.3 collective-permute-start.5
  90.7 5.4 %collective-permute-start.6 = (f32[4,1,32,128]{3,2,1,0:T(8,128)S(1)}, f32[4,1,32,128]{3,2,1,0:T(8,128)S(1)}, u32[]{:S(2)}, u32[]{:S(2)}) collective-permute-start(f32[4,1,32,128]{3,2,1,0:T(8,128)S(1)} %get-tuple-element.134), channel_id=1, source_target_pairs={{0,1},{1,2},{2,3},{3,4},{4,5},{5,6},{6,7},{8,9},{9,10},{10,11},{11... | collective-permute-start | bytes 196616 | tf_op jit(solution)/shard_map/ppermute | solution.py:19
  96.2 0.8 collective-permute-done.6
  97.3 1.3 collective-permute-start.7
  98.6 5.3 %collective-permute-start.8 = (f32[4,1,32,128]{3,2,1,0:T(8,128)S(1)}, f32[4,1,32,128]{3,2,1,0:T(8,128)S(1)}, u32[]{:S(2)}, u32[]{:S(2)}) collective-permute-start(f32[4,1,32,128]{3,2,1,0:T(8,128)S(1)} %get-tuple-element.128), channel_id=1, source_target_pairs={{0,1},{1,2},{2,3},{3,4},{4,5},{5,6},{6,7},{8,9},{9,10},{10,11},{11... | collective-permute-start | bytes 196616 | tf_op jit(solution)/shard_map/ppermute | solution.py:19
  104.0 0.8 collective-permute-done.8
  105.1 4.7 %collective-permute-start.10 = (f32[4,1,32,128]{3,2,1,0:T(8,128)S(1)}, f32[4,1,32,128]{3,2,1,0:T(8,128)S(1)}, u32[]{:S(2)}, u32[]{:S(2)}) collective-permute-start(f32[4,1,32,128]{3,2,1,0:T(8,128)S(1)} %get-tuple-element.126), channel_id=1, source_target_pairs={{0,1},{1,2},{2,3},{3,4},{4,5},{5,6},{6,7},{8,9},{9,10},{10,11},{11... | collective-permute-start | bytes 196616 | tf_op jit(solution)/shard_map/ppermute | solution.py:19
  109.8 1.3 collective-permute-start.9
  111.2 3.6 %collective-permute-done.9 = f32[4,1,32,128]{3,2,1,0:T(8,128)S(1)} collective-permute-done((f32[4,1,32,128]{3,2,1,0:T(8,128)S(1)}, f32[4,1,32,128]{3,2,1,0:T(8,128)S(1)}, u32[]{:S(2)}, u32[]{:S(2)}) %collective-permute-start.9) | collective-permute-done | bytes 65568 | tf_op jit(solution)/shard_map/ppermute | solution.py:21
  114.8 0.2 fusion.45
  114.9 0.8 copy-done.3
  115.9 40.9 %psum.33 = f32[3]{0:T(128)S(1)} all-reduce(f32[3]{0:T(128)S(1)} %fusion.1), channel_id=1, replica_groups=mesh['harm'=4,'slab'=8] {'harm','slab'}, use_global_device_ids=true, to_apply=%region_6.7 | all-reduce | flops 3 | bytes 24 | tf_op jit(solution)/shard_map/psum | solution.py:118
  157.0 0.6 multiply_reduce_fusion
  157.6 39.9 %psum.34 = f32[]{:T(128)} all-reduce(f32[]{:T(128)} %get-tuple-element.107), channel_id=1, replica_groups=mesh['harm'=4,'slab'=8] {'harm','slab'}, use_global_device_ids=true, to_apply=%region_9.10 | all-reduce | flops 1 | bytes 8 | tf_op jit(solution)/shard_map/psum | solution.py:120
  198.2 0.6 pad_maximum_fusion.13
  198.8 0.7 divide_bitcast_fusion
  (59 shorter events, 2.7 us)
Async XLA Ops:
  0.6 0.7 copy-start.5
  2.4 0.7 copy-start
  2.4 0.8 copy-start.4
  3.3 18.4 %copy-start.2 = (f32[4,2,32,128]{3,2,1,0:T(8,128)S(1)}, f32[4,2,32,128]{3,2,1,0:T(8,128)}, u32[]{:S(2)}) copy-start(f32[4,2,32,128]{3,2,1,0:T(8,128)} %copy-done) | copy-start | bytes 393220
  21.7 17.5 %collective-permute-start = (f32[4,2,32,128]{3,2,1,0:T(8,128)S(1)}, f32[4,2,32,128]{3,2,1,0:T(8,128)S(1)}, u32[]{:S(2)}, u32[]{:S(2)}) collective-permute-start(f32[4,2,32,128]{3,2,1,0:T(8,128)S(1)} %copy.11), channel_id=1, source_target_pairs={{0,8},{8,16},{16,24},{24,0},{1,9},{9,17},{17,25},{25,1},{2,10},{10... | collective-permute-start | bytes 393224 | tf_op jit(solution)/shard_map/while/body/eval_jaxpr/ppermute | solution.py:36
  39.3 17.5 %collective-permute-start = (f32[4,2,32,128]{3,2,1,0:T(8,128)S(1)}, f32[4,2,32,128]{3,2,1,0:T(8,128)S(1)}, u32[]{:S(2)}, u32[]{:S(2)}) collective-permute-start(f32[4,2,32,128]{3,2,1,0:T(8,128)S(1)} %copy.11), channel_id=1, source_target_pairs={{0,8},{8,16},{16,24},{24,0},{1,9},{9,17},{17,25},{25,1},{2,10},{10... | collective-permute-start | bytes 393224 | tf_op jit(solution)/shard_map/while/body/eval_jaxpr/ppermute | solution.py:36
  56.8 17.4 %collective-permute-start = (f32[4,2,32,128]{3,2,1,0:T(8,128)S(1)}, f32[4,2,32,128]{3,2,1,0:T(8,128)S(1)}, u32[]{:S(2)}, u32[]{:S(2)}) collective-permute-start(f32[4,2,32,128]{3,2,1,0:T(8,128)S(1)} %copy.11), channel_id=1, source_target_pairs={{0,8},{8,16},{16,24},{24,0},{1,9},{9,17},{17,25},{25,1},{2,10},{10... | collective-permute-start | bytes 393224 | tf_op jit(solution)/shard_map/while/body/eval_jaxpr/ppermute | solution.py:36
  74.3 0.9 copy-start.1
  75.2 5.7 %collective-permute-start.1 = (f32[16,1,32,128]{3,2,1,0:T(8,128)S(1)}, f32[16,1,32,128]{3,2,1,0:T(8,128)S(1)}, u32[]{:S(2)}, u32[]{:S(2)}) collective-permute-start(f32[16,1,32,128]{3,2,1,0:T(8,128)S(1)} %get-tuple-element.117), channel_id=1, source_target_pairs={{1,0},{2,1},{3,2},{4,3},{5,4},{6,5},{7,6},{9,8},{10,9},{11,10},{12... | collective-permute-start | bytes 786440 | tf_op jit(solution)/shard_map/ppermute | solution.py:21
  76.5 4.4 %collective-permute-start.2 = (f32[16,1,32,128]{3,2,1,0:T(8,128)S(1)}, f32[16,1,32,128]{3,2,1,0:T(8,128)S(1)}, u32[]{:S(2)}, u32[]{:S(2)}) collective-permute-start(f32[16,1,32,128]{3,2,1,0:T(8,128)S(1)} %get-tuple-element.118), channel_id=1, source_target_pairs={{0,1},{1,2},{2,3},{3,4},{4,5},{5,6},{6,7},{8,9},{9,10},{10,11},{11... | collective-permute-start | bytes 786440 | tf_op jit(solution)/shard_map/ppermute | solution.py:19
  81.2 7.1 %collective-permute-start.3 = (f32[4,1,32,128]{3,2,1,0:T(8,128)S(1)}, f32[4,1,32,128]{3,2,1,0:T(8,128)S(1)}, u32[]{:S(2)}, u32[]{:S(2)}) collective-permute-start(f32[4,1,32,128]{3,2,1,0:T(8,128)S(1)} %get-tuple-element.139), channel_id=1, source_target_pairs={{1,0},{2,1},{3,2},{4,3},{5,4},{6,5},{7,6},{9,8},{10,9},{11,10},{12... | collective-permute-start | bytes 196616 | tf_op jit(solution)/shard_map/ppermute | solution.py:21
  82.5 6.6 %collective-permute-start.4 = (f32[4,1,32,128]{3,2,1,0:T(8,128)S(1)}, f32[4,1,32,128]{3,2,1,0:T(8,128)S(1)}, u32[]{:S(2)}, u32[]{:S(2)}) collective-permute-start(f32[4,1,32,128]{3,2,1,0:T(8,128)S(1)} %get-tuple-element.140), channel_id=1, source_target_pairs={{0,1},{1,2},{2,3},{3,4},{4,5},{5,6},{6,7},{8,9},{9,10},{10,11},{11... | collective-permute-start | bytes 196616 | tf_op jit(solution)/shard_map/ppermute | solution.py:19
  89.4 6.9 %collective-permute-start.5 = (f32[4,1,32,128]{3,2,1,0:T(8,128)S(1)}, f32[4,1,32,128]{3,2,1,0:T(8,128)S(1)}, u32[]{:S(2)}, u32[]{:S(2)}) collective-permute-start(f32[4,1,32,128]{3,2,1,0:T(8,128)S(1)} %get-tuple-element.133), channel_id=1, source_target_pairs={{1,0},{2,1},{3,2},{4,3},{5,4},{6,5},{7,6},{9,8},{10,9},{11,10},{12... | collective-permute-start | bytes 196616 | tf_op jit(solution)/shard_map/ppermute | solution.py:21
  90.7 6.3 %collective-permute-start.6 = (f32[4,1,32,128]{3,2,1,0:T(8,128)S(1)}, f32[4,1,32,128]{3,2,1,0:T(8,128)S(1)}, u32[]{:S(2)}, u32[]{:S(2)}) collective-permute-start(f32[4,1,32,128]{3,2,1,0:T(8,128)S(1)} %get-tuple-element.134), channel_id=1, source_target_pairs={{0,1},{1,2},{2,3},{3,4},{4,5},{5,6},{6,7},{8,9},{9,10},{10,11},{11... | collective-permute-start | bytes 196616 | tf_op jit(solution)/shard_map/ppermute | solution.py:19
  97.3 6.7 %collective-permute-start.7 = (f32[4,1,32,128]{3,2,1,0:T(8,128)S(1)}, f32[4,1,32,128]{3,2,1,0:T(8,128)S(1)}, u32[]{:S(2)}, u32[]{:S(2)}) collective-permute-start(f32[4,1,32,128]{3,2,1,0:T(8,128)S(1)} %get-tuple-element.127), channel_id=1, source_target_pairs={{1,0},{2,1},{3,2},{4,3},{5,4},{6,5},{7,6},{9,8},{10,9},{11,10},{12... | collective-permute-start | bytes 196616 | tf_op jit(solution)/shard_map/ppermute | solution.py:21
  98.6 6.2 %collective-permute-start.8 = (f32[4,1,32,128]{3,2,1,0:T(8,128)S(1)}, f32[4,1,32,128]{3,2,1,0:T(8,128)S(1)}, u32[]{:S(2)}, u32[]{:S(2)}) collective-permute-start(f32[4,1,32,128]{3,2,1,0:T(8,128)S(1)} %get-tuple-element.128), channel_id=1, source_target_pairs={{0,1},{1,2},{2,3},{3,4},{4,5},{5,6},{6,7},{8,9},{9,10},{10,11},{11... | collective-permute-start | bytes 196616 | tf_op jit(solution)/shard_map/ppermute | solution.py:19
  105.1 6.1 %collective-permute-start.10 = (f32[4,1,32,128]{3,2,1,0:T(8,128)S(1)}, f32[4,1,32,128]{3,2,1,0:T(8,128)S(1)}, u32[]{:S(2)}, u32[]{:S(2)}) collective-permute-start(f32[4,1,32,128]{3,2,1,0:T(8,128)S(1)} %get-tuple-element.126), channel_id=1, source_target_pairs={{0,1},{1,2},{2,3},{3,4},{4,5},{5,6},{6,7},{8,9},{9,10},{10,11},{11... | collective-permute-start | bytes 196616 | tf_op jit(solution)/shard_map/ppermute | solution.py:19
  109.8 5.0 %collective-permute-start.9 = (f32[4,1,32,128]{3,2,1,0:T(8,128)S(1)}, f32[4,1,32,128]{3,2,1,0:T(8,128)S(1)}, u32[]{:S(2)}, u32[]{:S(2)}) collective-permute-start(f32[4,1,32,128]{3,2,1,0:T(8,128)S(1)} %get-tuple-element.125), channel_id=1, source_target_pairs={{1,0},{2,1},{3,2},{4,3},{5,4},{6,5},{7,6},{9,8},{10,9},{11,10},{12... | collective-permute-start | bytes 196616 | tf_op jit(solution)/shard_map/ppermute | solution.py:21
  114.8 1.0 copy-start.3
where the time goes:
time: 200 us; the launch traced here: 199 us
  blocking collectives  151 us (76%)
  starting transfers between devices  30.8 us (15%)
  waiting for transfers between devices  5.94 us (3%)
  other arithmetic  4.62 us (2%)
  local copies, waits for them, and re-layouts  4.36 us (2%)
  between operations  2.59 us (1%)
    psum x4, blocking collectives, broadcast(): return lax.psum(jnp.where(mine, x, jnp.zeros_like(x)), axis)  70 us
    psum x1, blocking collectives, shards(): projection = lax.psum(local_proj, ('harm', 'slab')) / entries  40.9 us
    psum x1, blocking collectives, shards(): square = lax.psum(jnp.sum(residue * residue), ('harm', 'slab')) / entries  39.9 us
    ppermute x5, starting transfers between devices, padded_2(): lax.ppermute(tail, axis, [(i, (i + 1) % count) for i in range(ends)])  24.2 us
    ppermute x5, starting transfers between devices, padded_2(): lax.ppermute(head, axis, [((i + 1) % count, i) for i in range(ends)])  6.46 us
  transfers between devices with their start and end apart: 13, of which 4 were waited for; matrix products, arithmetic and copies ran while one was open for 1% of the time, Pallas kernels for 0%

commit v1 on v0

--- a/solution.py
+++ b/solution.py
@@ -115,7 +115,7 @@
         * cell_shape[3]
     )
     local_proj = jnp.sum(vectors * solution[None], axis=(1, 2, 3, 4))
-    projection = lax.psum(local_proj, ("harm", "slab")) / entries
+    projection = jnp.sum(lax.all_gather(local_proj, ("harm", "slab")), axis=0) / entries
     residue = solution - jnp.sum(projection[:, None, None, None, None] * vectors, axis=0)
     square = lax.psum(jnp.sum(residue * residue), ("harm", "slab")) / entries
     norm_value = jnp.sqrt(square + epsilon)

time: 200 us -> 201 us (level)
    unnamed x0 -> x1, blocking collectives: none -> 40.9 us
    psum x1 -> x0, blocking collectives: 40.9 us -> none  [shards(): projection = lax.psum(local_proj, ('harm', 'slab')) / entries]
where the time goes in v1:
time: 201 us; the launch traced here: 200 us
  blocking collectives  151 us (75%)
  starting transfers between devices  30.8 us (15%)
  waiting for transfers between devices  5.94 us (3%)
  local copies, waits for them, and re-layouts  4.68 us (2%)
  other arithmetic  4.65 us (2%)
  between operations  2.61 us (1%)
    psum x4, blocking collectives, broadcast(): return lax.psum(jnp.where(mine, x, jnp.zeros_like(x)), axis)  70 us
    unnamed x1, blocking collectives  40.9 us
    psum x1, blocking collectives, shards(): square = lax.psum(jnp.sum(residue * residue), ('harm', 'slab')) / entries  39.9 us
    ppermute x5, starting transfers between devices, padded_2(): lax.ppermute(tail, axis, [(i, (i + 1) % count) for i in range(ends)])  24.2 us
    ppermute x5, starting transfers between devices, padded_2(): lax.ppermute(head, axis, [((i + 1) % count, i) for i in range(ends)])  6.46 us
  transfers between devices with their start and end apart: 13, of which 4 were waited for; matrix products, arithmetic and copies ran while one was open for 1% of the time, Pallas kernels for 0%

profile of v1, /device:TPU:0, one launch (start us, length us, event | category | flops | bytes accessed | tf_op | source)
XLA Modules:
  0.0 199.9 jit_solution(7748662336502036259)
XLA Ops:
  0.7 0.6 copy-done.5
  1.3 1.1 fusion
  2.4 0.6 copy-done
  3.1 0.2 copy-done.4
  3.3 18.4 %psum.25 = bf16[3,2,32,128]{3,2,1,0:T(8,128)(2,1)S(1)} all-reduce(bf16[3,2,32,128]{3,2,1,0:T(8,128)(2,1)S(1)} %broadcast_select_fusion.1), channel_id=1, replica_groups=mesh['harm'=4,'slab'=8] {'harm'}, use_global_device_ids=true, to_apply=%region_4.5 | all-reduce | flops 24576 | bytes 98304 | tf_op jit(solution)/shard_map/psum | solution.py:30
  21.7 52.6 %while.16 = (s32[]{:T(128)}, f32[3,4,2,32,128]{4,3,2,1,0:T(8,128)S(1)}, f32[4,2,32,128]{3,2,1,0:T(8,128)S(1)}, bf16[3,2,32,128]{3,2,1,0:T(8,128)(2,1)S(1)}, s32[]{:T(128)}, /*index=5*/u32[]{:T(128)}, s32[]{:T(128)}) while((s32[]{:T(128)}, f32[3,4,2,32,128]{4,3,2,1,0:T(8,128)S(1)}, f32[4,2,32,128]{3,2,1,0:T(8,128)S(1)}, ...), condition=%wide.region_3.4_spmd.clone, body=%wide.region_1.3_spmd.clone.sunk | while | flops 368647 | bytes 2146473 | solution.py:99
  21.8 17.2 %psum.29 = bf16[3,2,32,128]{3,2,1,0:T(8,128)(2,1)S(1)} all-reduce(bf16[3,2,32,128]{3,2,1,0:T(8,128)(2,1)S(1)} %broadcast_select_fusion.3), channel_id=1, replica_groups=mesh['harm'=4,'slab'=8] {'harm'}, use_global_device_ids=true, to_apply=%region_2.2 | all-reduce | flops 24576 | bytes 98304 | tf_op jit(solution)/shard_map/while/body/eval_jaxpr/psum | solution.py:30
  39.4 17.3 %psum.29 = bf16[3,2,32,128]{3,2,1,0:T(8,128)(2,1)S(1)} all-reduce(bf16[3,2,32,128]{3,2,1,0:T(8,128)(2,1)S(1)} %broadcast_select_fusion.3), channel_id=1, replica_groups=mesh['harm'=4,'slab'=8] {'harm'}, use_global_device_ids=true, to_apply=%region_2.2 | all-reduce | flops 24576 | bytes 98304 | tf_op jit(solution)/shard_map/while/body/eval_jaxpr/psum | solution.py:30
  56.9 17.1 %psum.29 = bf16[3,2,32,128]{3,2,1,0:T(8,128)(2,1)S(1)} all-reduce(bf16[3,2,32,128]{3,2,1,0:T(8,128)(2,1)S(1)} %broadcast_select_fusion.3), channel_id=1, replica_groups=mesh['harm'=4,'slab'=8] {'harm'}, use_global_device_ids=true, to_apply=%region_2.2 | all-reduce | flops 24576 | bytes 98304 | tf_op jit(solution)/shard_map/while/body/eval_jaxpr/psum | solution.py:30
  74.3 0.8 copy-done.1
  75.2 1.3 collective-permute-start.1
  76.5 3.0 %collective-permute-start.2 = (f32[16,1,32,128]{3,2,1,0:T(8,128)S(1)}, f32[16,1,32,128]{3,2,1,0:T(8,128)S(1)}, u32[]{:S(2)}, u32[]{:S(2)}) collective-permute-start(f32[16,1,32,128]{3,2,1,0:T(8,128)S(1)} %get-tuple-element.118), channel_id=1, source_target_pairs={{0,1},{1,2},{2,3},{3,4},{4,5},{5,6},{6,7},{8,9},{9,10},{10,11},{11... | collective-permute-start | bytes 786440 | tf_op jit(solution)/shard_map/ppermute | solution.py:19
  80.9 0.2 broadcast_divide_fusion
  81.2 1.3 collective-permute-start.3
  82.5 5.7 %collective-permute-start.4 = (f32[4,1,32,128]{3,2,1,0:T(8,128)S(1)}, f32[4,1,32,128]{3,2,1,0:T(8,128)S(1)}, u32[]{:S(2)}, u32[]{:S(2)}) collective-permute-start(f32[4,1,32,128]{3,2,1,0:T(8,128)S(1)} %get-tuple-element.140), channel_id=1, source_target_pairs={{0,1},{1,2},{2,3},{3,4},{4,5},{5,6},{6,7},{8,9},{9,10},{10,11},{11... | collective-permute-start | bytes 196616 | tf_op jit(solution)/shard_map/ppermute | solution.py:19
  88.3 0.8 collective-permute-done.4
  89.4 1.3 collective-permute-start.5
  90.7 5.4 %collective-permute-start.6 = (f32[4,1,32,128]{3,2,1,0:T(8,128)S(1)}, f32[4,1,32,128]{3,2,1,0:T(8,128)S(1)}, u32[]{:S(2)}, u32[]{:S(2)}) collective-permute-start(f32[4,1,32,128]{3,2,1,0:T(8,128)S(1)} %get-tuple-element.134), channel_id=1, source_target_pairs={{0,1},{1,2},{2,3},{3,4},{4,5},{5,6},{6,7},{8,9},{9,10},{10,11},{11... | collective-permute-start | bytes 196616 | tf_op jit(solution)/shard_map/ppermute | solution.py:19
  96.2 0.8 collective-permute-done.6
  97.3 1.3 collective-permute-start.7
  98.6 5.3 %collective-permute-start.8 = (f32[4,1,32,128]{3,2,1,0:T(8,128)S(1)}, f32[4,1,32,128]{3,2,1,0:T(8,128)S(1)}, u32[]{:S(2)}, u32[]{:S(2)}) collective-permute-start(f32[4,1,32,128]{3,2,1,0:T(8,128)S(1)} %get-tuple-element.128), channel_id=1, source_target_pairs={{0,1},{1,2},{2,3},{3,4},{4,5},{5,6},{6,7},{8,9},{9,10},{10,11},{11... | collective-permute-start | bytes 196616 | tf_op jit(solution)/shard_map/ppermute | solution.py:19
  104.0 0.8 collective-permute-done.8
  105.1 4.7 %collective-permute-start.10 = (f32[4,1,32,128]{3,2,1,0:T(8,128)S(1)}, f32[4,1,32,128]{3,2,1,0:T(8,128)S(1)}, u32[]{:S(2)}, u32[]{:S(2)}) collective-permute-start(f32[4,1,32,128]{3,2,1,0:T(8,128)S(1)} %get-tuple-element.126), channel_id=1, source_target_pairs={{0,1},{1,2},{2,3},{3,4},{4,5},{5,6},{6,7},{8,9},{9,10},{10,11},{11... | collective-permute-start | bytes 196616 | tf_op jit(solution)/shard_map/ppermute | solution.py:19
  109.8 1.3 collective-permute-start.9
  111.2 3.6 %collective-permute-done.9 = f32[4,1,32,128]{3,2,1,0:T(8,128)S(1)} collective-permute-done((f32[4,1,32,128]{3,2,1,0:T(8,128)S(1)}, f32[4,1,32,128]{3,2,1,0:T(8,128)S(1)}, u32[]{:S(2)}, u32[]{:S(2)}) %collective-permute-start.9) | collective-permute-done | bytes 65568 | tf_op jit(solution)/shard_map/ppermute | solution.py:21
  114.9 0.8 copy-done.3
  115.9 0.2 dynamic-update-slice
  116.1 40.9 %all-reduce.6 = f32[96]{0:T(128)S(1)} all-reduce(f32[96]{0:T(128)S(1)} %dynamic-update-slice), channel_id=2, replica_groups=mesh['harm'=4,'slab'=8] {'harm','slab'}, use_global_device_ids=true, to_apply=%add.6 | all-reduce | flops 96 | bytes 768
  157.3 0.6 multiply_reduce_fusion
  158.0 39.9 %psum.26 = f32[]{:T(128)} all-reduce(f32[]{:T(128)} %get-tuple-element.107), channel_id=1, replica_groups=mesh['harm'=4,'slab'=8] {'harm','slab'}, use_global_device_ids=true, to_apply=%region_9.10 | all-reduce | flops 1 | bytes 8 | tf_op jit(solution)/shard_map/psum | solution.py:120
  198.6 0.6 pad_maximum_fusion.13
  199.2 0.7 divide_bitcast_fusion
  (63 shorter events, 2.9 us)
Async XLA Ops:
  0.6 0.7 copy-start.5
  2.4 0.7 copy-start
  2.4 0.8 copy-start.4
  3.3 18.4 %copy-start.2 = (f32[4,2,32,128]{3,2,1,0:T(8,128)S(1)}, f32[4,2,32,128]{3,2,1,0:T(8,128)}, u32[]{:S(2)}) copy-start(f32[4,2,32,128]{3,2,1,0:T(8,128)} %copy-done) | copy-start | bytes 393220
  21.7 17.5 %collective-permute-start = (f32[4,2,32,128]{3,2,1,0:T(8,128)S(1)}, f32[4,2,32,128]{3,2,1,0:T(8,128)S(1)}, u32[]{:S(2)}, u32[]{:S(2)}) collective-permute-start(f32[4,2,32,128]{3,2,1,0:T(8,128)S(1)} %copy.11), channel_id=1, source_target_pairs={{0,8},{8,16},{16,24},{24,0},{1,9},{9,17},{17,25},{25,1},{2,10},{10... | collective-permute-start | bytes 393224 | tf_op jit(solution)/shard_map/while/body/eval_jaxpr/ppermute | solution.py:36
  39.3 17.5 %collective-permute-start = (f32[4,2,32,128]{3,2,1,0:T(8,128)S(1)}, f32[4,2,32,128]{3,2,1,0:T(8,128)S(1)}, u32[]{:S(2)}, u32[]{:S(2)}) collective-permute-start(f32[4,2,32,128]{3,2,1,0:T(8,128)S(1)} %copy.11), channel_id=1, source_target_pairs={{0,8},{8,16},{16,24},{24,0},{1,9},{9,17},{17,25},{25,1},{2,10},{10... | collective-permute-start | bytes 393224 | tf_op jit(solution)/shard_map/while/body/eval_jaxpr/ppermute | solution.py:36
  56.8 17.4 %collective-permute-start = (f32[4,2,32,128]{3,2,1,0:T(8,128)S(1)}, f32[4,2,32,128]{3,2,1,0:T(8,128)S(1)}, u32[]{:S(2)}, u32[]{:S(2)}) collective-permute-start(f32[4,2,32,128]{3,2,1,0:T(8,128)S(1)} %copy.11), channel_id=1, source_target_pairs={{0,8},{8,16},{16,24},{24,0},{1,9},{9,17},{17,25},{25,1},{2,10},{10... | collective-permute-start | bytes 393224 | tf_op jit(solution)/shard_map/while/body/eval_jaxpr/ppermute | solution.py:36
  74.3 0.9 copy-start.1
  75.2 5.7 %collective-permute-start.1 = (f32[16,1,32,128]{3,2,1,0:T(8,128)S(1)}, f32[16,1,32,128]{3,2,1,0:T(8,128)S(1)}, u32[]{:S(2)}, u32[]{:S(2)}) collective-permute-start(f32[16,1,32,128]{3,2,1,0:T(8,128)S(1)} %get-tuple-element.117), channel_id=1, source_target_pairs={{1,0},{2,1},{3,2},{4,3},{5,4},{6,5},{7,6},{9,8},{10,9},{11,10},{12... | collective-permute-start | bytes 786440 | tf_op jit(solution)/shard_map/ppermute | solution.py:21
  76.5 4.4 %collective-permute-start.2 = (f32[16,1,32,128]{3,2,1,0:T(8,128)S(1)}, f32[16,1,32,128]{3,2,1,0:T(8,128)S(1)}, u32[]{:S(2)}, u32[]{:S(2)}) collective-permute-start(f32[16,1,32,128]{3,2,1,0:T(8,128)S(1)} %get-tuple-element.118), channel_id=1, source_target_pairs={{0,1},{1,2},{2,3},{3,4},{4,5},{5,6},{6,7},{8,9},{9,10},{10,11},{11... | collective-permute-start | bytes 786440 | tf_op jit(solution)/shard_map/ppermute | solution.py:19
  81.2 7.1 %collective-permute-start.3 = (f32[4,1,32,128]{3,2,1,0:T(8,128)S(1)}, f32[4,1,32,128]{3,2,1,0:T(8,128)S(1)}, u32[]{:S(2)}, u32[]{:S(2)}) collective-permute-start(f32[4,1,32,128]{3,2,1,0:T(8,128)S(1)} %get-tuple-element.139), channel_id=1, source_target_pairs={{1,0},{2,1},{3,2},{4,3},{5,4},{6,5},{7,6},{9,8},{10,9},{11,10},{12... | collective-permute-start | bytes 196616 | tf_op jit(solution)/shard_map/ppermute | solution.py:21
  82.5 6.6 %collective-permute-start.4 = (f32[4,1,32,128]{3,2,1,0:T(8,128)S(1)}, f32[4,1,32,128]{3,2,1,0:T(8,128)S(1)}, u32[]{:S(2)}, u32[]{:S(2)}) collective-permute-start(f32[4,1,32,128]{3,2,1,0:T(8,128)S(1)} %get-tuple-element.140), channel_id=1, source_target_pairs={{0,1},{1,2},{2,3},{3,4},{4,5},{5,6},{6,7},{8,9},{9,10},{10,11},{11... | collective-permute-start | bytes 196616 | tf_op jit(solution)/shard_map/ppermute | solution.py:19
  89.4 6.9 %collective-permute-start.5 = (f32[4,1,32,128]{3,2,1,0:T(8,128)S(1)}, f32[4,1,32,128]{3,2,1,0:T(8,128)S(1)}, u32[]{:S(2)}, u32[]{:S(2)}) collective-permute-start(f32[4,1,32,128]{3,2,1,0:T(8,128)S(1)} %get-tuple-element.133), channel_id=1, source_target_pairs={{1,0},{2,1},{3,2},{4,3},{5,4},{6,5},{7,6},{9,8},{10,9},{11,10},{12... | collective-permute-start | bytes 196616 | tf_op jit(solution)/shard_map/ppermute | solution.py:21
  90.7 6.3 %collective-permute-start.6 = (f32[4,1,32,128]{3,2,1,0:T(8,128)S(1)}, f32[4,1,32,128]{3,2,1,0:T(8,128)S(1)}, u32[]{:S(2)}, u32[]{:S(2)}) collective-permute-start(f32[4,1,32,128]{3,2,1,0:T(8,128)S(1)} %get-tuple-element.134), channel_id=1, source_target_pairs={{0,1},{1,2},{2,3},{3,4},{4,5},{5,6},{6,7},{8,9},{9,10},{10,11},{11... | collective-permute-start | bytes 196616 | tf_op jit(solution)/shard_map/ppermute | solution.py:19
  97.3 6.7 %collective-permute-start.7 = (f32[4,1,32,128]{3,2,1,0:T(8,128)S(1)}, f32[4,1,32,128]{3,2,1,0:T(8,128)S(1)}, u32[]{:S(2)}, u32[]{:S(2)}) collective-permute-start(f32[4,1,32,128]{3,2,1,0:T(8,128)S(1)} %get-tuple-element.127), channel_id=1, source_target_pairs={{1,0},{2,1},{3,2},{4,3},{5,4},{6,5},{7,6},{9,8},{10,9},{11,10},{12... | collective-permute-start | bytes 196616 | tf_op jit(solution)/shard_map/ppermute | solution.py:21
  98.6 6.2 %collective-permute-start.8 = (f32[4,1,32,128]{3,2,1,0:T(8,128)S(1)}, f32[4,1,32,128]{3,2,1,0:T(8,128)S(1)}, u32[]{:S(2)}, u32[]{:S(2)}) collective-permute-start(f32[4,1,32,128]{3,2,1,0:T(8,128)S(1)} %get-tuple-element.128), channel_id=1, source_target_pairs={{0,1},{1,2},{2,3},{3,4},{4,5},{5,6},{6,7},{8,9},{9,10},{10,11},{11... | collective-permute-start | bytes 196616 | tf_op jit(solution)/shard_map/ppermute | solution.py:19
  105.1 6.1 %collective-permute-start.10 = (f32[4,1,32,128]{3,2,1,0:T(8,128)S(1)}, f32[4,1,32,128]{3,2,1,0:T(8,128)S(1)}, u32[]{:S(2)}, u32[]{:S(2)}) collective-permute-start(f32[4,1,32,128]{3,2,1,0:T(8,128)S(1)} %get-tuple-element.126), channel_id=1, source_target_pairs={{0,1},{1,2},{2,3},{3,4},{4,5},{5,6},{6,7},{8,9},{9,10},{10,11},{11... | collective-permute-start | bytes 196616 | tf_op jit(solution)/shard_map/ppermute | solution.py:19
  109.8 5.0 %collective-permute-start.9 = (f32[4,1,32,128]{3,2,1,0:T(8,128)S(1)}, f32[4,1,32,128]{3,2,1,0:T(8,128)S(1)}, u32[]{:S(2)}, u32[]{:S(2)}) collective-permute-start(f32[4,1,32,128]{3,2,1,0:T(8,128)S(1)} %get-tuple-element.125), channel_id=1, source_target_pairs={{1,0},{2,1},{3,2},{4,3},{5,4},{6,5},{7,6},{9,8},{10,9},{11,10},{12... | collective-permute-start | bytes 196616 | tf_op jit(solution)/shard_map/ppermute | solution.py:21
  114.8 1.0 copy-start.3
